TPU v7x, 32 devices: a whole 2x2x4 slice. The times are simulated.
32 devices in a mesh: dp: 4 (over z), seq: 8 (over y, x, core).
Axes of the slice: x: 2, y: 2, z: 4, core: 2. Of those that a mesh axis runs over, the one named last changes fastest.
Arguments:
- query_rows: bfloat16 [4, 3072, 1024], P('dp', 'seq'), may hold values from -48 to 48
- key_rows: bfloat16 [4, 3072, 1024], P('dp', 'seq'), may hold values from -8 to 8
- value_rows: bfloat16 [4, 3072, 1024], P('dp', 'seq'), may hold values from -6 to 6
- scale_end: int32 [3072], P('seq'), may hold values from 1 to 3072, as said below
- out_weight: bfloat16 [1024, 2048], replicated, may hold values from -0.8984375 to 0.8984375
- grad_out: bfloat16 [4, 3072, 2048], P('dp', 'seq'), may hold values from -1.5 to 1.5
Outputs:
- mixed_out: bfloat16 [4, 3072, 2048], P('dp', 'seq')
- out_grad: float32 [1024, 2048], P(('dp', 'seq'))
Inputs may be any that keep to these rules, and one draw needn't show every extreme that they name: scale_end is constant over each of 4 scales of consecutive tokens, equals the index one past the scale's last token (so scale_end[t] > t), never falls, and is 3072 on the last scale; the same for every image.
All inputs are finite; a program needn't handle non-finite values.
Results may differ from a plain program's by a relative error of at most 0.014.
Values may be sent and summed in bfloat16 or wider, within the bound.
No kernel may reach another device: no remote copies, remote signals or barrier semaphores. Data moves between devices by JAX's collectives and lax.ppermute only.
A program may use at most 256 MiB of HBM per device.

v0:
```python
import functools

import jax
import jax.numpy as jnp
from jax import lax
from jax.experimental import pallas as pl
from jax.experimental.pallas import tpu as pltpu
from jax.sharding import PartitionSpec as P


HEAD = 128
FLOOR = -1e30
SCALES = 4
LOG2E = 1.4426950408889634


HBM = pl.BlockSpec(memory_space=pltpu.HBM)
VMEM = pl.BlockSpec(memory_space=pltpu.VMEM)
SMEM = pl.BlockSpec(memory_space=pltpu.SMEM)


def place():
    index = lax.axis_index("seq")
    return index // 2, index % 2


def params(mebibytes):
    return pltpu.CompilerParams(vmem_limit_bytes=mebibytes * 1024 * 1024)


def cut(sources, chips, width):
    row_count = sources[0].shape[0]
    count = len(sources)

    def kernel(*refs):
        ins, outs, sems = refs[:count], refs[count:-1], refs[-1]
        chip, _ = place()
        copies = []
        for away in reversed(range(chips)):
            columns = pl.ds(pl.multiple_of((chip ^ away) * width, width), width)
            for at, source in enumerate(ins):
                copies.append(
                    pltpu.make_async_copy(
                        source.at[:, columns],
                        outs[away].at[:, at * width : (at + 1) * width],
                        sems.at[len(copies)],
                    )
                )
        for copy in copies:
            copy.start()
        for copy in copies:
            copy.wait()

    shape = jax.ShapeDtypeStruct((row_count, count * width), sources[0].dtype)
    return pl.pallas_call(
        kernel,
        out_shape=[shape] * chips,
        in_specs=[HBM] * count,
        out_specs=[VMEM] * chips,
        scratch_shapes=[pltpu.SemaphoreType.DMA((count * chips,))],
        compiler_params=params(16),
        name="cut",
    )(*sources)


def assemble(near, far, chips):
    row_count, wide = near[0].shape

    def kernel(*refs):
        pieces, out = (refs[:chips], refs[chips : 2 * chips]), refs[2 * chips]
        chip, core = place()
        for away in range(chips):
            for side in range(2):
                at = (chip ^ away) * 2 + (core ^ side)
                rows = pl.ds(pl.multiple_of(at * row_count, row_count), row_count)
                out[rows, :] = pieces[side][away][...]

    return pl.pallas_call(
        kernel,
        out_shape=jax.ShapeDtypeStruct((2 * chips * row_count, wide), near[0].dtype),
        in_specs=[VMEM] * (2 * chips),
        out_specs=VMEM,
        compiler_params=params(16),
        name="assemble",
    )(*near, *far)


def attend(queries, ends, aways, both, width):
    row_count = queries[0].shape[0]
    total = both.shape[0]
    heads = width // HEAD
    count = len(queries)
    choices = 4
    step_k = total // choices
    scale = float(HEAD) ** -0.5 * LOG2E

    def kernel(*refs):
        ends_in = refs[:count]
        q_in = refs[count : 2 * count]
        both_ref = refs[2 * count]
        outs = refs[2 * count + 1 : 3 * count + 1]
        qbuf, obuf, sbuf = refs[3 * count + 1 :]
        chip, core = place()

        def block(index, starts, limits, steps):
            token = starts + lax.broadcasted_iota(jnp.int32, (row_count, HEAD), 0)
            limit = jnp.full((row_count, HEAD), limits[-1], jnp.int32)
            for value in reversed(limits[:-1]):
                limit = jnp.where(token < value, value, limit)
            room = limit - lax.broadcasted_iota(jnp.int32, (row_count, HEAD), 1)
            shifts = []
            for head in range(heads):
                columns = slice(head * HEAD, (head + 1) * HEAD)
                query = qbuf[index, :, columns]
                top = None
                for at in range(0, steps * step_k, step_k):
                    score = lax.dot_general(
                        query,
                        both_ref[at : at + step_k, columns],
                        (((1,), (1,)), ((), ())),
                        preferred_element_type=jnp.float32,
                    )
                    for base in range(0, step_k, HEAD):
                        part = jnp.where(room > at + base, score[:, base : base + HEAD], FLOOR)
                        sbuf[head, :, at + base : at + base + HEAD] = part
                        top = part if top is None else jnp.maximum(top, part)
                shifts.append(jnp.max(top, axis=1, keepdims=True) * scale)
            for head in range(heads):
                columns = slice(head * HEAD, (head + 1) * HEAD)
                tally = acc = None
                for at in range(0, steps * step_k, step_k):
                    weights = jnp.exp2(sbuf[head, :, at : at + step_k] * scale - shifts[head])
                    for base in range(0, step_k, HEAD):
                        part = weights[:, base : base + HEAD]
                        tally = part if tally is None else tally + part
                    product = jnp.dot(
                        weights.astype(jnp.bfloat16),
                        both_ref[at : at + step_k, width + head * HEAD : width + (head + 1) * HEAD],
                        preferred_element_type=jnp.float32,
                    )
                    acc = product if acc is None else acc + product
                obuf[index, :, columns] = (acc / jnp.sum(tally, axis=1, keepdims=True)).astype(
                    obuf.dtype
                )

        starts, limits = [], []
        for index, away in enumerate(aways):
            qbuf[index] = q_in[index][...]
            start = ((chip ^ away) * 2 + core) * row_count
            limit = [ends_in[index][0]]
            for _ in range(SCALES - 1):
                limit.append(ends_in[index][jnp.minimum(limit[-1] - start, row_count - 1)])
            starts.append(start)
            limits.append(limit)

        def turn(index, carry):
            def pick(values):
                value = values[0]
                for at in range(1, count):
                    value = jnp.where(index == at, values[at], value)
                return value

            start = pick(starts)
            limit = [pick([one[at] for one in limits]) for at in range(SCALES)]
            needed = (limit[-1] + step_k - 1) // step_k
            for steps in range(1, choices + 1):

                @pl.when(needed == steps)
                def _(steps=steps):
                    block(index, start, limit, steps)

            return carry

        lax.fori_loop(0, count, turn, 0)
        for index in range(count):
            outs[index][...] = obuf[index]

    return pl.pallas_call(
        kernel,
        out_shape=[jax.ShapeDtypeStruct((row_count, width), jnp.bfloat16)] * count,
        in_specs=[SMEM] * count + [VMEM] * (count + 1),
        out_specs=[VMEM] * count,
        scratch_shapes=[
            pltpu.VMEM((count, row_count, width), jnp.bfloat16),
            pltpu.VMEM((count, row_count, width), jnp.bfloat16),
            pltpu.VMEM((heads, row_count, total), jnp.float32),
        ],
        compiler_params=params(30),
        cost_estimate=pl.CostEstimate(
            flops=4 * count * row_count * total * width,
            bytes_accessed=4 * total * width,
            transcendentals=count * row_count * total * heads,
        ),
        name="attend",
    )(*ends, *queries, both)


def weight_gradient(near, far, grad_near, grad_far, chips, width, planes, split):
    row_count = near[0].shape[0]
    full = chips * width
    out_width = grad_near.shape[1]
    group = full // (planes * chips * 2)

    def kernel(*refs):
        pieces = (refs[0:chips], refs[chips : 2 * chips])
        grads = refs[2 * chips : 2 * chips + 2]
        by_plane = refs[2 * chips + 2 : 2 * chips + 2 + planes]
        by_chip = refs[2 * chips + 2 + planes : 3 * chips + 2 + planes]
        turned, left = refs[3 * chips + 2 + planes :]
        chip, core = place()
        here = lax.axis_index("dp")
        for side in range(2):
            for away in range(chips):
                start = pl.multiple_of((chip ^ away) * width, width)
                turned[pl.ds(start, width), side * row_count : (side + 1) * row_count] = (
                    pieces[side][away][...].T
                )

        def product(outs, columns, picks):
            for out, starts in zip(outs, picks):
                for at, start in enumerate(starts):
                    rows = pl.ds(pl.multiple_of((start * 2 + core) * group, group), group)
                    left[at * group : (at + 1) * group, :] = turned[rows, :]
                size = len(starts) * group
                value = jnp.dot(
                    left[:size, :row_count], grads[0][:, columns], preferred_element_type=jnp.float32
                ) + jnp.dot(
                    left[:size, row_count:], grads[1][:, columns], preferred_element_type=jnp.float32
                )
                out[...] = value.astype(out.dtype)

        product(
            by_plane,
            slice(split, out_width),
            [[(here ^ far_) * chips + at for at in range(chips)] for far_ in range(planes)],
        )
        product(
            by_chip,
            slice(0, split),
            [[at * chips + (chip ^ far_) for at in range(planes)] for far_ in range(chips)],
        )

    def shape(rows, columns, away):
        return jax.ShapeDtypeStruct((rows, columns), jnp.float32 if away == 0 else jnp.bfloat16)

    outs = pl.pallas_call(
        kernel,
        out_shape=[shape(chips * group, out_width - split, away) for away in range(planes)]
        + [shape(planes * group, split, away) for away in range(chips)],
        in_specs=[VMEM] * (2 * chips + 2),
        out_specs=[VMEM] * (planes + chips),
        scratch_shapes=[
            pltpu.VMEM((full, 2 * row_count), jnp.bfloat16),
            pltpu.VMEM((max(planes, chips) * group, 2 * row_count), jnp.bfloat16),
        ],
        compiler_params=params(32),
        cost_estimate=pl.CostEstimate(
            flops=2 * full * row_count * out_width,
            bytes_accessed=4 * row_count * out_width,
            transcendentals=0,
        ),
        name="weight_gradient",
    )(*near, *far, grad_near, grad_far)
    return outs[:planes], outs[planes:]


def project(pieces, out_weight, chips, width):
    row_count = pieces[0].shape[0]
    out_width = out_weight.shape[1]

    def kernel(*refs):
        ins, weight, out = refs[:chips], refs[chips], refs[chips + 1]
        chip, _ = place()
        step = min(out_width, 512)
        for column in range(0, out_width, step):
            value = None
            for away in range(chips):
                start = pl.multiple_of((chip ^ away) * width, width)
                part = jnp.dot(
                    ins[away][...],
                    weight[pl.ds(start, width), column : column + step],
                    preferred_element_type=jnp.float32,
                )
                value = part if value is None else value + part
            out[:, column : column + step] = value.astype(out.dtype)

    return pl.pallas_call(
        kernel,
        out_shape=jax.ShapeDtypeStruct((row_count, out_width), jnp.bfloat16),
        in_specs=[VMEM] * (chips + 1),
        out_specs=VMEM,
        compiler_params=params(24),
        cost_estimate=pl.CostEstimate(
            flops=2 * row_count * out_weight.size,
            bytes_accessed=2 * out_weight.size,
            transcendentals=0,
        ),
        name="project",
    )(*pieces, out_weight)


def add_up(own, others, axis, size):
    group = own.shape[0] // size

    def kernel(*refs):
        ins, outs = refs[: 1 + len(others)], refs[1 + len(others) :]
        here = lax.axis_index("dp") if axis == "dp" else place()[0]
        for away in range(size):
            rows = pl.ds(pl.multiple_of((here ^ away) * group, group), group)
            value = ins[0][rows, :]
            for ref in ins[1:]:
                value = value + ref[rows, :].astype(jnp.float32)
            outs[away][...] = value.astype(outs[away].dtype)

    return pl.pallas_call(
        kernel,
        out_shape=[
            jax.ShapeDtypeStruct(
                (group, own.shape[1]), jnp.float32 if away == 0 else jnp.bfloat16
            )
            for away in range(size)
        ],
        in_specs=[VMEM] * (1 + len(others)),
        out_specs=[VMEM] * size,
        compiler_params=params(16),
        name="add_up",
    )(own, *others)


def finish(lefts, rights):
    rows, split = lefts[0].shape
    width = split + rights[0].shape[1]

    def kernel(*refs):
        ins, out = refs[:-1], refs[-1]
        for group, columns in (
            (ins[: len(lefts)], slice(0, split)),
            (ins[len(lefts) :], slice(split, width)),
        ):
            value = group[0][...]
            for ref in group[1:]:
                value = value + ref[...].astype(jnp.float32)
            out[:, columns] = value

    return pl.pallas_call(
        kernel,
        out_shape=jax.ShapeDtypeStruct((rows, width), jnp.float32),
        in_specs=[VMEM] * (len(lefts) + len(rights)),
        out_specs=VMEM,
        compiler_params=params(16),
        name="finish",
    )(*lefts, *rights)


def body(seq, planes, query_rows, key_rows, value_rows, scale_end, out_weight, grad_out):
    chips = seq // 2
    full = query_rows.shape[2]
    width = full // chips

    def over(axis, size, value, mask):
        return lax.ppermute(value, axis, [(i, i ^ mask) for i in range(size)])

    def other_core(value):
        return over("seq", seq, value, 1)

    def spread(pieces):
        return [pieces[0]] + [over("seq", seq, pieces[away], 2 * away) for away in range(1, chips)]

    def meet(pieces):
        return [pieces[0]] + [over("dp", planes, pieces[away], away) for away in range(1, planes)]

    near = spread(cut([key_rows[0], value_rows[0]], chips, width))
    queries = spread(cut([query_rows[0]], chips, width))
    ends = spread([scale_end] * chips)
    far = [other_core(piece) for piece in near]
    grad_near = grad_out[0]
    grad_far = other_core(grad_near)
    both = assemble(near, far, chips)
    mine = [None] * chips
    for aways in (list(range(chips - 1)), [chips - 1]):
        results = attend([queries[i] for i in aways], [ends[i] for i in aways], aways, both, width)
        for away, piece in zip(aways, results):
            mine[away] = over("seq", seq, piece, 2 * away) if away else piece
    others = [other_core(piece) for piece in mine]
    out_width = out_weight.shape[1]
    split = out_width * 5 // 8
    by_plane, by_chip = weight_gradient(
        mine, others, grad_near, grad_far, chips, width, planes, split
    )
    met = meet(by_plane)
    gathered = spread(by_chip)
    mixed_out = project(mine, out_weight, chips, width)[None]
    lefts = meet(add_up(gathered[0], gathered[1:], "dp", planes))
    rights = spread(add_up(met[0], met[1:], "seq", chips))
    return mixed_out, finish(lefts, rights)


def solution(mesh):
    placed = (
        P("dp", "seq", None),
        P("dp", "seq", None),
        P("dp", "seq", None),
        P("seq"),
        P(),
        P("dp", "seq", None),
    )
    seq, planes = mesh.shape["seq"], mesh.shape["dp"]
    return jax.shard_map(
        functools.partial(body, seq, planes),
        mesh=mesh,
        in_specs=placed,
        out_specs=(P("dp", "seq", None), P(("dp", "seq"), None)),
        check_vma=False,
    )
```

profile of v0, /device:TPU:0, one launch (start us, length us, event | category | flops | bytes accessed | tf_op | source)
XLA Modules:
  0.0 105.8 jit_solution(16139168140573957815)
XLA Ops:
  0.7 1.1 %copy-done.1 = bf16[1,384,1024]{2,1,0:T(8,128)(2,1)S(1)} copy-done((bf16[1,384,1024]{2,1,0:T(8,128)(2,1)S(1)}, bf16[1,384,1024]{2,1,0:T(8,128)(2,1)}, u32[]{:S(2)}) %copy-start.1) | copy-done | bytes 786456
  1.8 1.1 %copy-done.2 = bf16[1,384,1024]{2,1,0:T(8,128)(2,1)S(1)} copy-done((bf16[1,384,1024]{2,1,0:T(8,128)(2,1)S(1)}, bf16[1,384,1024]{2,1,0:T(8,128)(2,1)}, u32[]{:S(2)}) %copy-start.2) | copy-done | bytes 786456
  3.2 4.0 %collective-permute-start.6 = (bf16[384,512]{1,0:T(8,128)(2,1)S(1)}, bf16[384,512]{1,0:T(8,128)(2,1)S(1)}, u32[]{:S(2)}, u32[]{:S(2)}) collective-permute-start(bf16[384,512]{1,0:T(8,128)(2,1)S(1)} %get-tuple-element.35), channel_id=1, source_target_pairs={{0,6},{1,7},{2,4},{3,5},{4,2},{5,3},{6,0},{7,1},{8,14},{9,15},{10,... | collective-permute-start | bytes 1179656 | tf_op jit(solution)/shard_map/ppermute | solution.py:361
  7.2 0.5 collective-permute-start.4
  8.4 8.9 %collective-permute-done.6.refs_3_ = bf16[384,512]{1,0:T(8,128)(2,1)S(1)} collective-permute-done((bf16[384,512]{1,0:T(8,128)(2,1)S(1)}, bf16[384,512]{1,0:T(8,128)(2,1)S(1)}, u32[]{:S(2)}, u32[]{:S(2)}) %collective-permute-start.6) | collective-permute-done | bytes 393248 | tf_op jit(solution)/shard_map/ppermute | solution.py:361
  17.2 7.8 %collective-permute-done.4.refs_1_ = bf16[384,512]{1,0:T(8,128)(2,1)S(1)} collective-permute-done((bf16[384,512]{1,0:T(8,128)(2,1)S(1)}, bf16[384,512]{1,0:T(8,128)(2,1)S(1)}, u32[]{:S(2)}, u32[]{:S(2)}) %collective-permute-start.4) | collective-permute-done | bytes 393248 | tf_op jit(solution)/shard_map/ppermute | solution.py:361
  25.7 1.6 %collective-permute-start.2 = (bf16[384,256]{1,0:T(8,128)(2,1)S(1)}, bf16[384,256]{1,0:T(8,128)(2,1)S(1)}, u32[]{:S(2)}, u32[]{:S(2)}) collective-permute-start(bf16[384,256]{1,0:T(8,128)(2,1)S(1)} %get-tuple-element.30), channel_id=1, source_target_pairs={{0,2},{1,3},{2,0},{3,1},{4,6},{5,7},{6,4},{7,5},{8,10},{9,11},{10,... | collective-permute-start | bytes 589832 | tf_op jit(solution)/shard_map/ppermute | solution.py:361
  27.3 0.9 collective-permute-start.3
  28.2 0.5 collective-permute-start
  28.8 1.1 %collective-permute-start.1 = (s32[384]{0:T(512)S(1)}, s32[384]{0:T(512)S(1)}, u32[]{:S(2)}, u32[]{:S(2)}) collective-permute-start(s32[384]{0:T(512)S(1)} %copy-done.5), channel_id=1, source_target_pairs={{0,4},{1,5},{2,6},{3,7},{4,0},{5,1},{6,2},{7,3},{8,12},{9,13},{10,... | collective-permute-start | bytes 4616 | tf_op jit(solution)/shard_map/ppermute | solution.py:361
  30.1 2.6 %collective-permute-done.refs_1_ = s32[384]{0:T(512)S(1)} collective-permute-done((s32[384]{0:T(512)S(1)}, s32[384]{0:T(512)S(1)}, u32[]{:S(2)}, u32[]{:S(2)}) %collective-permute-start) | collective-permute-done | bytes 1568 | tf_op jit(solution)/shard_map/ppermute | solution.py:361
  32.7 2.3 %collective-permute-start.13 = (s32[384]{0:T(512)S(1)}, s32[384]{0:T(512)S(1)}, u32[]{:S(2)}, u32[]{:S(2)}) collective-permute-start(s32[384]{0:T(512)S(1)} %copy-done.5), channel_id=1, source_target_pairs={{0,6},{1,7},{2,4},{3,5},{4,2},{5,3},{6,0},{7,1},{8,14},{9,15},{10,... | collective-permute-start | bytes 4616 | tf_op jit(solution)/shard_map/ppermute | solution.py:361
  35.0 0.6 collective-permute-start.14
  35.6 11.6 %attend.2 = (bf16[384,256]{1,0:T(8,128)(2,1)S(1)}, bf16[384,256]{1,0:T(8,128)(2,1)S(1)}, bf16[384,256]{1,0:T(8,128)(2,1)S(1)}) custom-call(s32[384]{0:T(512)S(1)} %copy-done.5, s32[384]{0:T(512)S(1)} %collective-permute-done.refs_1_, s32[384]{0:T(512)S(1)} %collective-permute-done.1.refs_2_, bf16[384,256]{1,0:T(8,128)(2,1)S(1)} %get-tuple-element.29.refs_3_, ...), custom_call_target="tpu_custom_call" | custom-call | flops 3623878656 | bytes 3145728 | tf_op jit(solution)/shard_map/attend/pallas_call | solution.py:178
  47.2 1.6 %collective-permute-start.11 = (bf16[384,256]{1,0:T(8,128)(2,1)S(1)}, bf16[384,256]{1,0:T(8,128)(2,1)S(1)}, u32[]{:S(2)}, u32[]{:S(2)}) collective-permute-start(bf16[384,256]{1,0:T(8,128)(2,1)S(1)} %get-tuple-element.37), channel_id=1, source_target_pairs={{0,2},{1,3},{2,0},{3,1},{4,6},{5,7},{6,4},{7,5},{8,10},{9,11},{10,... | collective-permute-start | bytes 589832 | tf_op jit(solution)/shard_map/ppermute | solution.py:361
  48.8 3.6 %collective-permute-start.12 = (bf16[384,256]{1,0:T(8,128)(2,1)S(1)}, bf16[384,256]{1,0:T(8,128)(2,1)S(1)}, u32[]{:S(2)}, u32[]{:S(2)}) collective-permute-start(bf16[384,256]{1,0:T(8,128)(2,1)S(1)} %get-tuple-element.38), channel_id=1, source_target_pairs={{0,4},{1,5},{2,6},{3,7},{4,0},{5,1},{6,2},{7,3},{8,12},{9,13},{10,... | collective-permute-start | bytes 589832 | tf_op jit(solution)/shard_map/ppermute | solution.py:361
  52.4 5.4 %attend.3 = bf16[384,256]{1,0:T(8,128)(2,1)S(1)} custom-call(s32[384]{0:T(512)S(1)} %collective-permute-done.13.refs_0_, bf16[384,256]{1,0:T(8,128)(2,1)S(1)} %collective-permute-done.14.refs_1_, bf16[3072,512]{1,0:T(8,128)(2,1)S(1)} %assemble.1.refs_6_.refs_2_), custom_call_target="tpu_custom_call" | custom-call | flops 1207959552 | bytes 3145728 | tf_op jit(solution)/shard_map/attend/pallas_call | solution.py:178
  58.5 5.9 %collective-permute-done.15.refs_3_ = bf16[384,256]{1,0:T(8,128)(2,1)S(1)} collective-permute-done((bf16[384,256]{1,0:T(8,128)(2,1)S(1)}, bf16[384,256]{1,0:T(8,128)(2,1)S(1)}, u32[]{:S(2)}, u32[]{:S(2)}) %collective-permute-start.15) | collective-permute-done | bytes 196640 | tf_op jit(solution)/shard_map/ppermute | solution.py:361
  64.5 1.4 %collective-permute-done.19.refs_7_ = bf16[384,256]{1,0:T(8,128)(2,1)S(1)} collective-permute-done((bf16[384,256]{1,0:T(8,128)(2,1)S(1)}, bf16[384,256]{1,0:T(8,128)(2,1)S(1)}, u32[]{:S(2)}, u32[]{:S(2)}) %collective-permute-start.19) | collective-permute-done | bytes 196640 | tf_op jit(solution)/shard_map/ppermute | solution.py:361
  65.9 2.8 %weight_gradient.1 = (f32[128,768]{1,0:T(8,128)S(1)}, bf16[128,768]{1,0:T(8,128)(2,1)S(1)}, bf16[128,768]{1,0:T(8,128)(2,1)S(1)}, bf16[128,768]{1,0:T(8,128)(2,1...) custom-call(bf16[384,256]{1,0:T(8,128)(2,1)S(1)} %get-tuple-element., ...), custom_call_target="tpu_custom_call" | custom-call | flops 1610612736 | bytes 3145728 | tf_op jit(solution)/shard_map/weight_gradient/pallas_call | solution.py:246
  68.7 1.6 %collective-permute-start.27 = (bf16[128,768]{1,0:T(8,128)(2,1)S(1)}, bf16[128,768]{1,0:T(8,128)(2,1)S(1)}, u32[]{:S(2)}, u32[]{:S(2)}) collective-permute-start(bf16[128,768]{1,0:T(8,128)(2,1)S(1)} %get-tuple-element.49), channel_id=1, source_target_pairs={{0,8},{8,0},{16,24},{24,16},{1,9},{9,1},{17,25},{25,17},{2,10},{10... | collective-permute-start | bytes 589832 | tf_op jit(solution)/shard_map/ppermute | solution.py:361
  70.9 2.9 %collective-permute-start.23 = (bf16[128,1280]{1,0:T(8,128)(2,1)S(1)}, bf16[128,1280]{1,0:T(8,128)(2,1)S(1)}, u32[]{:S(2)}, u32[]{:S(2)}) collective-permute-start(bf16[128,1280]{1,0:T(8,128)(2,1)S(1)} %get-tuple-element.43), channel_id=1, source_target_pairs={{0,6},{1,7},{2,4},{3,5},{4,2},{5,3},{6,0},{7,1},{8,14},{9,15},{10,... | collective-permute-start | bytes 983048 | tf_op jit(solution)/shard_map/ppermute | solution.py:361
  73.9 2.6 %collective-permute-start.28 = (bf16[128,768]{1,0:T(8,128)(2,1)S(1)}, bf16[128,768]{1,0:T(8,128)(2,1)S(1)}, u32[]{:S(2)}, u32[]{:S(2)}) collective-permute-start(bf16[128,768]{1,0:T(8,128)(2,1)S(1)} %get-tuple-element.50), channel_id=1, source_target_pairs={{0,16},{8,24},{16,0},{24,8},{1,17},{9,25},{17,1},{25,9},{2,18},{10... | collective-permute-start | bytes 589832 | tf_op jit(solution)/shard_map/ppermute | solution.py:361
  76.5 4.0 %collective-permute-start.29 = (bf16[128,768]{1,0:T(8,128)(2,1)S(1)}, bf16[128,768]{1,0:T(8,128)(2,1)S(1)}, u32[]{:S(2)}, u32[]{:S(2)}) collective-permute-start(bf16[128,768]{1,0:T(8,128)(2,1)S(1)} %get-tuple-element.51), channel_id=1, source_target_pairs={{0,24},{8,16},{16,8},{24,0},{1,25},{9,17},{17,9},{25,1},{2,26},{10... | collective-permute-start | bytes 589832 | tf_op jit(solution)/shard_map/ppermute | solution.py:361
  80.4 9.8 %collective-permute-done.28.refs_2_ = bf16[128,768]{1,0:T(8,128)(2,1)S(1)} collective-permute-done((bf16[128,768]{1,0:T(8,128)(2,1)S(1)}, bf16[128,768]{1,0:T(8,128)(2,1)S(1)}, u32[]{:S(2)}, u32[]{:S(2)}) %collective-permute-start.28) | collective-permute-done | bytes 196640 | tf_op jit(solution)/shard_map/ppermute | solution.py:361
  91.0 2.9 %collective-permute-start.32 = (bf16[32,768]{1,0:T(8,128)(2,1)S(1)}, bf16[32,768]{1,0:T(8,128)(2,1)S(1)}, u32[]{:S(2)}, u32[]{:S(2)}) collective-permute-start(bf16[32,768]{1,0:T(8,128)(2,1)S(1)} %get-tuple-element.55), channel_id=1, source_target_pairs={{0,6},{1,7},{2,4},{3,5},{4,2},{5,3},{6,0},{7,1},{8,14},{9,15},{10,... | collective-permute-start | bytes 147464 | tf_op jit(solution)/shard_map/ppermute | solution.py:361
  94.1 3.6 %collective-permute-start.24 = (bf16[32,1280]{1,0:T(8,128)(2,1)S(1)}, bf16[32,1280]{1,0:T(8,128)(2,1)S(1)}, u32[]{:S(2)}, u32[]{:S(2)}) collective-permute-start(bf16[32,1280]{1,0:T(8,128)(2,1)S(1)} %get-tuple-element.45), channel_id=1, source_target_pairs={{0,8},{8,0},{16,24},{24,16},{1,9},{9,1},{17,25},{25,17},{2,10},{10... | collective-permute-start | bytes 245768 | tf_op jit(solution)/shard_map/ppermute | solution.py:361
  97.6 1.1 %collective-permute-start.25 = (bf16[32,1280]{1,0:T(8,128)(2,1)S(1)}, bf16[32,1280]{1,0:T(8,128)(2,1)S(1)}, u32[]{:S(2)}, u32[]{:S(2)}) collective-permute-start(bf16[32,1280]{1,0:T(8,128)(2,1)S(1)} %get-tuple-element.46), channel_id=1, source_target_pairs={{0,16},{8,24},{16,0},{24,8},{1,17},{9,25},{17,1},{25,9},{2,18},{10... | collective-permute-start | bytes 245768 | tf_op jit(solution)/shard_map/ppermute | solution.py:361
  98.8 1.4 %collective-permute-start.26 = (bf16[32,1280]{1,0:T(8,128)(2,1)S(1)}, bf16[32,1280]{1,0:T(8,128)(2,1)S(1)}, u32[]{:S(2)}, u32[]{:S(2)}) collective-permute-start(bf16[32,1280]{1,0:T(8,128)(2,1)S(1)} %get-tuple-element.47), channel_id=1, source_target_pairs={{0,24},{8,16},{16,8},{24,0},{1,25},{9,17},{17,9},{25,1},{2,26},{10... | collective-permute-start | bytes 245768 | tf_op jit(solution)/shard_map/ppermute | solution.py:361
  100.2 2.9 %project.1 = bf16[384,2048]{1,0:T(8,128)(2,1)} custom-call(bf16[384,256]{1,0:T(8,128)(2,1)S(1)} %get-tuple-element.36.refs_0_, bf16[384,256]{1,0:T(8,128)(2,1)S(1)} %collective-permute-done.11.refs_1_, bf16[384,256]{1,0:T(8,128)(2,1)S(1)} %collective-permute-done.12.refs_2_, bf16[384,256]{1,0:T(8,128)(2,1)S(1)} %collective-permute-done.15.refs_3_, ...), custom_call_target="tpu_custom_call" | custom-call | flops 1610612736 | bytes 4194304 | tf_op jit(solution)/shard_map/project/pallas_call | solution.py:287
  103.1 1.9 %collective-permute-done.25.refs_2_ = bf16[32,1280]{1,0:T(8,128)(2,1)S(1)} collective-permute-done((bf16[32,1280]{1,0:T(8,128)(2,1)S(1)}, bf16[32,1280]{1,0:T(8,128)(2,1)S(1)}, u32[]{:S(2)}, u32[]{:S(2)}) %collective-permute-start.25) | collective-permute-done | bytes 81952 | tf_op jit(solution)/shard_map/ppermute | solution.py:361
  105.1 0.8 finish.1
  (56 shorter events, 4.0 us)
Async XLA Ops:
  3.2 14.0 %collective-permute-start.6 = (bf16[384,512]{1,0:T(8,128)(2,1)S(1)}, bf16[384,512]{1,0:T(8,128)(2,1)S(1)}, u32[]{:S(2)}, u32[]{:S(2)}) collective-permute-start(bf16[384,512]{1,0:T(8,128)(2,1)S(1)} %get-tuple-element.35), channel_id=1, source_target_pairs={{0,6},{1,7},{2,4},{3,5},{4,2},{5,3},{6,0},{7,1},{8,14},{9,15},{10,... | collective-permute-start | bytes 1179656 | tf_op jit(solution)/shard_map/ppermute | solution.py:361
  7.2 17.8 %collective-permute-start.4 = (bf16[384,512]{1,0:T(8,128)(2,1)S(1)}, bf16[384,512]{1,0:T(8,128)(2,1)S(1)}, u32[]{:S(2)}, u32[]{:S(2)}) collective-permute-start(bf16[384,512]{1,0:T(8,128)(2,1)S(1)} %get-tuple-element.33), channel_id=1, source_target_pairs={{0,2},{1,3},{2,0},{3,1},{4,6},{5,7},{6,4},{7,5},{8,10},{9,11},{10,... | collective-permute-start | bytes 1179656 | tf_op jit(solution)/shard_map/ppermute | solution.py:361
  7.7 17.3 %collective-permute-start.5 = (bf16[384,512]{1,0:T(8,128)(2,1)S(1)}, bf16[384,512]{1,0:T(8,128)(2,1)S(1)}, u32[]{:S(2)}, u32[]{:S(2)}) collective-permute-start(bf16[384,512]{1,0:T(8,128)(2,1)S(1)} %get-tuple-element.34), channel_id=1, source_target_pairs={{0,4},{1,5},{2,6},{3,7},{4,0},{5,1},{6,2},{7,3},{8,12},{9,13},{10,... | collective-permute-start | bytes 1179656 | tf_op jit(solution)/shard_map/ppermute | solution.py:361
  7.9 58.0 %collective-permute-start.20 = (bf16[384,2048]{1,0:T(8,128)(2,1)}, bf16[384,2048]{1,0:T(8,128)(2,1)S(1)}, u32[]{:S(2)}, u32[]{:S(2)}) collective-permute-start(bf16[384,2048]{1,0:T(8,128)(2,1)} %bitcast.8), channel_id=1, source_target_pairs={{0,1},{1,0},{2,3},{3,2},{4,5},{5,4},{6,7},{7,6},{8,9},{9,8},{10,11... | collective-permute-start | bytes 4718600 | tf_op jit(solution)/shard_map/ppermute | solution.py:361
  7.9 17.9 %collective-permute-start.7 = (bf16[384,512]{1,0:T(8,128)(2,1)S(1)}, bf16[384,512]{1,0:T(8,128)(2,1)S(1)}, u32[]{:S(2)}, u32[]{:S(2)}) collective-permute-start(bf16[384,512]{1,0:T(8,128)(2,1)S(1)} %get-tuple-element.32.refs_0_), channel_id=1, source_target_pairs={{0,1},{1,0},{2,3},{3,2},{4,5},{5,4},{6,7},{7,6},{8,9},{9,8},{10,11... | collective-permute-start | bytes 1179656 | tf_op jit(solution)/shard_map/ppermute | solution.py:361
  17.2 10.1 %collective-permute-start.10 = (bf16[384,512]{1,0:T(8,128)(2,1)S(1)}, bf16[384,512]{1,0:T(8,128)(2,1)S(1)}, u32[]{:S(2)}, u32[]{:S(2)}) collective-permute-start(bf16[384,512]{1,0:T(8,128)(2,1)S(1)} %collective-permute-done.6.refs_3_), channel_id=1, source_target_pairs={{0,1},{1,0},{2,3},{3,2},{4,5},{5,4},{6,7},{7,6},{8,9},{9,8},{10,11... | collective-permute-start | bytes 1179656 | tf_op jit(solution)/shard_map/ppermute | solution.py:361
  25.0 3.2 %collective-permute-start.8 = (bf16[384,512]{1,0:T(8,128)(2,1)S(1)}, bf16[384,512]{1,0:T(8,128)(2,1)S(1)}, u32[]{:S(2)}, u32[]{:S(2)}) collective-permute-start(bf16[384,512]{1,0:T(8,128)(2,1)S(1)} %collective-permute-done.4.refs_1_), channel_id=1, source_target_pairs={{0,1},{1,0},{2,3},{3,2},{4,5},{5,4},{6,7},{7,6},{8,9},{9,8},{10,11... | collective-permute-start | bytes 1179656 | tf_op jit(solution)/shard_map/ppermute | solution.py:361
  25.1 3.7 %collective-permute-start.9 = (bf16[384,512]{1,0:T(8,128)(2,1)S(1)}, bf16[384,512]{1,0:T(8,128)(2,1)S(1)}, u32[]{:S(2)}, u32[]{:S(2)}) collective-permute-start(bf16[384,512]{1,0:T(8,128)(2,1)S(1)} %collective-permute-done.5.refs_2_), channel_id=1, source_target_pairs={{0,1},{1,0},{2,3},{3,2},{4,5},{5,4},{6,7},{7,6},{8,9},{9,8},{10,11... | collective-permute-start | bytes 1179656 | tf_op jit(solution)/shard_map/ppermute | solution.py:361
  25.7 9.9 %collective-permute-start.2 = (bf16[384,256]{1,0:T(8,128)(2,1)S(1)}, bf16[384,256]{1,0:T(8,128)(2,1)S(1)}, u32[]{:S(2)}, u32[]{:S(2)}) collective-permute-start(bf16[384,256]{1,0:T(8,128)(2,1)S(1)} %get-tuple-element.30), channel_id=1, source_target_pairs={{0,2},{1,3},{2,0},{3,1},{4,6},{5,7},{6,4},{7,5},{8,10},{9,11},{10,... | collective-permute-start | bytes 589832 | tf_op jit(solution)/shard_map/ppermute | solution.py:361
  27.3 8.3 %collective-permute-start.3 = (bf16[384,256]{1,0:T(8,128)(2,1)S(1)}, bf16[384,256]{1,0:T(8,128)(2,1)S(1)}, u32[]{:S(2)}, u32[]{:S(2)}) collective-permute-start(bf16[384,256]{1,0:T(8,128)(2,1)S(1)} %get-tuple-element.31), channel_id=1, source_target_pairs={{0,4},{1,5},{2,6},{3,7},{4,0},{5,1},{6,2},{7,3},{8,12},{9,13},{10,... | collective-permute-start | bytes 589832 | tf_op jit(solution)/shard_map/ppermute | solution.py:361
  28.2 4.5 %collective-permute-start = (s32[384]{0:T(512)S(1)}, s32[384]{0:T(512)S(1)}, u32[]{:S(2)}, u32[]{:S(2)}) collective-permute-start(s32[384]{0:T(512)S(1)} %copy-done.5), channel_id=1, source_target_pairs={{0,2},{1,3},{2,0},{3,1},{4,6},{5,7},{6,4},{7,5},{8,10},{9,11},{10,... | collective-permute-start | bytes 4616 | tf_op jit(solution)/shard_map/ppermute | solution.py:361
  28.8 6.2 %collective-permute-start.1 = (s32[384]{0:T(512)S(1)}, s32[384]{0:T(512)S(1)}, u32[]{:S(2)}, u32[]{:S(2)}) collective-permute-start(s32[384]{0:T(512)S(1)} %copy-done.5), channel_id=1, source_target_pairs={{0,4},{1,5},{2,6},{3,7},{4,0},{5,1},{6,2},{7,3},{8,12},{9,13},{10,... | collective-permute-start | bytes 4616 | tf_op jit(solution)/shard_map/ppermute | solution.py:361
  32.7 19.7 %collective-permute-start.13 = (s32[384]{0:T(512)S(1)}, s32[384]{0:T(512)S(1)}, u32[]{:S(2)}, u32[]{:S(2)}) collective-permute-start(s32[384]{0:T(512)S(1)} %copy-done.5), channel_id=1, source_target_pairs={{0,6},{1,7},{2,4},{3,5},{4,2},{5,3},{6,0},{7,1},{8,14},{9,15},{10,... | collective-permute-start | bytes 4616 | tf_op jit(solution)/shard_map/ppermute | solution.py:361
  35.0 17.4 %collective-permute-start.14 = (bf16[384,256]{1,0:T(8,128)(2,1)S(1)}, bf16[384,256]{1,0:T(8,128)(2,1)S(1)}, u32[]{:S(2)}, u32[]{:S(2)}) collective-permute-start(bf16[384,256]{1,0:T(8,128)(2,1)S(1)} %get-tuple-element.39), channel_id=1, source_target_pairs={{0,6},{1,7},{2,4},{3,5},{4,2},{5,3},{6,0},{7,1},{8,14},{9,15},{10,... | collective-permute-start | bytes 589832 | tf_op jit(solution)/shard_map/ppermute | solution.py:361
  47.2 10.7 %collective-permute-start.11 = (bf16[384,256]{1,0:T(8,128)(2,1)S(1)}, bf16[384,256]{1,0:T(8,128)(2,1)S(1)}, u32[]{:S(2)}, u32[]{:S(2)}) collective-permute-start(bf16[384,256]{1,0:T(8,128)(2,1)S(1)} %get-tuple-element.37), channel_id=1, source_target_pairs={{0,2},{1,3},{2,0},{3,1},{4,6},{5,7},{6,4},{7,5},{8,10},{9,11},{10,... | collective-permute-start | bytes 589832 | tf_op jit(solution)/shard_map/ppermute | solution.py:361
  48.8 9.7 %collective-permute-start.12 = (bf16[384,256]{1,0:T(8,128)(2,1)S(1)}, bf16[384,256]{1,0:T(8,128)(2,1)S(1)}, u32[]{:S(2)}, u32[]{:S(2)}) collective-permute-start(bf16[384,256]{1,0:T(8,128)(2,1)S(1)} %get-tuple-element.38), channel_id=1, source_target_pairs={{0,4},{1,5},{2,6},{3,7},{4,0},{5,1},{6,2},{7,3},{8,12},{9,13},{10,... | collective-permute-start | bytes 589832 | tf_op jit(solution)/shard_map/ppermute | solution.py:361
  57.8 6.6 %collective-permute-start.15 = (bf16[384,256]{1,0:T(8,128)(2,1)S(1)}, bf16[384,256]{1,0:T(8,128)(2,1)S(1)}, u32[]{:S(2)}, u32[]{:S(2)}) collective-permute-start(bf16[384,256]{1,0:T(8,128)(2,1)S(1)} %attend.3), channel_id=1, source_target_pairs={{0,6},{1,7},{2,4},{3,5},{4,2},{5,3},{6,0},{7,1},{8,14},{9,15},{10,... | collective-permute-start | bytes 589832 | tf_op jit(solution)/shard_map/ppermute | solution.py:361
  57.9 6.6 %collective-permute-start.16 = (bf16[384,256]{1,0:T(8,128)(2,1)S(1)}, bf16[384,256]{1,0:T(8,128)(2,1)S(1)}, u32[]{:S(2)}, u32[]{:S(2)}) collective-permute-start(bf16[384,256]{1,0:T(8,128)(2,1)S(1)} %get-tuple-element.36.refs_0_), channel_id=1, source_target_pairs={{0,1},{1,0},{2,3},{3,2},{4,5},{5,4},{6,7},{7,6},{8,9},{9,8},{10,11... | collective-permute-start | bytes 589832 | tf_op jit(solution)/shard_map/ppermute | solution.py:361
  58.0 6.5 %collective-permute-start.17 = (bf16[384,256]{1,0:T(8,128)(2,1)S(1)}, bf16[384,256]{1,0:T(8,128)(2,1)S(1)}, u32[]{:S(2)}, u32[]{:S(2)}) collective-permute-start(bf16[384,256]{1,0:T(8,128)(2,1)S(1)} %collective-permute-done.11.refs_1_), channel_id=1, source_target_pairs={{0,1},{1,0},{2,3},{3,2},{4,5},{5,4},{6,7},{7,6},{8,9},{9,8},{10,11... | collective-permute-start | bytes 589832 | tf_op jit(solution)/shard_map/ppermute | solution.py:361
  58.5 6.0 %collective-permute-start.18 = (bf16[384,256]{1,0:T(8,128)(2,1)S(1)}, bf16[384,256]{1,0:T(8,128)(2,1)S(1)}, u32[]{:S(2)}, u32[]{:S(2)}) collective-permute-start(bf16[384,256]{1,0:T(8,128)(2,1)S(1)} %collective-permute-done.12.refs_2_), channel_id=1, source_target_pairs={{0,1},{1,0},{2,3},{3,2},{4,5},{5,4},{6,7},{7,6},{8,9},{9,8},{10,11... | collective-permute-start | bytes 589832 | tf_op jit(solution)/shard_map/ppermute | solution.py:361
  68.7 7.7 %collective-permute-start.27 = (bf16[128,768]{1,0:T(8,128)(2,1)S(1)}, bf16[128,768]{1,0:T(8,128)(2,1)S(1)}, u32[]{:S(2)}, u32[]{:S(2)}) collective-permute-start(bf16[128,768]{1,0:T(8,128)(2,1)S(1)} %get-tuple-element.49), channel_id=1, source_target_pairs={{0,8},{8,0},{16,24},{24,16},{1,9},{9,1},{17,25},{25,17},{2,10},{10... | collective-permute-start | bytes 589832 | tf_op jit(solution)/shard_map/ppermute | solution.py:361
  70.4 20.6 %collective-permute-start.21 = (bf16[128,1280]{1,0:T(8,128)(2,1)S(1)}, bf16[128,1280]{1,0:T(8,128)(2,1)S(1)}, u32[]{:S(2)}, u32[]{:S(2)}) collective-permute-start(bf16[128,1280]{1,0:T(8,128)(2,1)S(1)} %get-tuple-element.41), channel_id=1, source_target_pairs={{0,2},{1,3},{2,0},{3,1},{4,6},{5,7},{6,4},{7,5},{8,10},{9,11},{10,... | collective-permute-start | bytes 983048 | tf_op jit(solution)/shard_map/ppermute | solution.py:361
  70.5 23.4 %collective-permute-start.22 = (bf16[128,1280]{1,0:T(8,128)(2,1)S(1)}, bf16[128,1280]{1,0:T(8,128)(2,1)S(1)}, u32[]{:S(2)}, u32[]{:S(2)}) collective-permute-start(bf16[128,1280]{1,0:T(8,128)(2,1)S(1)} %get-tuple-element.42), channel_id=1, source_target_pairs={{0,4},{1,5},{2,6},{3,7},{4,0},{5,1},{6,2},{7,3},{8,12},{9,13},{10,... | collective-permute-start | bytes 983048 | tf_op jit(solution)/shard_map/ppermute | solution.py:361
  70.9 23.0 %collective-permute-start.23 = (bf16[128,1280]{1,0:T(8,128)(2,1)S(1)}, bf16[128,1280]{1,0:T(8,128)(2,1)S(1)}, u32[]{:S(2)}, u32[]{:S(2)}) collective-permute-start(bf16[128,1280]{1,0:T(8,128)(2,1)S(1)} %get-tuple-element.43), channel_id=1, source_target_pairs={{0,6},{1,7},{2,4},{3,5},{4,2},{5,3},{6,0},{7,1},{8,14},{9,15},{10,... | collective-permute-start | bytes 983048 | tf_op jit(solution)/shard_map/ppermute | solution.py:361
  73.9 16.4 %collective-permute-start.28 = (bf16[128,768]{1,0:T(8,128)(2,1)S(1)}, bf16[128,768]{1,0:T(8,128)(2,1)S(1)}, u32[]{:S(2)}, u32[]{:S(2)}) collective-permute-start(bf16[128,768]{1,0:T(8,128)(2,1)S(1)} %get-tuple-element.50), channel_id=1, source_target_pairs={{0,16},{8,24},{16,0},{24,8},{1,17},{9,25},{17,1},{25,9},{2,18},{10... | collective-permute-start | bytes 589832 | tf_op jit(solution)/shard_map/ppermute | solution.py:361
  76.5 13.8 %collective-permute-start.29 = (bf16[128,768]{1,0:T(8,128)(2,1)S(1)}, bf16[128,768]{1,0:T(8,128)(2,1)S(1)}, u32[]{:S(2)}, u32[]{:S(2)}) collective-permute-start(bf16[128,768]{1,0:T(8,128)(2,1)S(1)} %get-tuple-element.51), channel_id=1, source_target_pairs={{0,24},{8,16},{16,8},{24,0},{1,25},{9,17},{17,9},{25,1},{2,26},{10... | collective-permute-start | bytes 589832 | tf_op jit(solution)/shard_map/ppermute | solution.py:361
  90.3 8.4 %collective-permute-start.30 = (bf16[32,768]{1,0:T(8,128)(2,1)S(1)}, bf16[32,768]{1,0:T(8,128)(2,1)S(1)}, u32[]{:S(2)}, u32[]{:S(2)}) collective-permute-start(bf16[32,768]{1,0:T(8,128)(2,1)S(1)} %get-tuple-element.53), channel_id=1, source_target_pairs={{0,2},{1,3},{2,0},{3,1},{4,6},{5,7},{6,4},{7,5},{8,10},{9,11},{10,... | collective-permute-start | bytes 147464 | tf_op jit(solution)/shard_map/ppermute | solution.py:361
  90.5 12.6 %collective-permute-start.31 = (bf16[32,768]{1,0:T(8,128)(2,1)S(1)}, bf16[32,768]{1,0:T(8,128)(2,1)S(1)}, u32[]{:S(2)}, u32[]{:S(2)}) collective-permute-start(bf16[32,768]{1,0:T(8,128)(2,1)S(1)} %get-tuple-element.54), channel_id=1, source_target_pairs={{0,4},{1,5},{2,6},{3,7},{4,0},{5,1},{6,2},{7,3},{8,12},{9,13},{10,... | collective-permute-start | bytes 147464 | tf_op jit(solution)/shard_map/ppermute | solution.py:361
  91.0 12.1 %collective-permute-start.32 = (bf16[32,768]{1,0:T(8,128)(2,1)S(1)}, bf16[32,768]{1,0:T(8,128)(2,1)S(1)}, u32[]{:S(2)}, u32[]{:S(2)}) collective-permute-start(bf16[32,768]{1,0:T(8,128)(2,1)S(1)} %get-tuple-element.55), channel_id=1, source_target_pairs={{0,6},{1,7},{2,4},{3,5},{4,2},{5,3},{6,0},{7,1},{8,14},{9,15},{10,... | collective-permute-start | bytes 147464 | tf_op jit(solution)/shard_map/ppermute | solution.py:361
  94.1 9.1 %collective-permute-start.24 = (bf16[32,1280]{1,0:T(8,128)(2,1)S(1)}, bf16[32,1280]{1,0:T(8,128)(2,1)S(1)}, u32[]{:S(2)}, u32[]{:S(2)}) collective-permute-start(bf16[32,1280]{1,0:T(8,128)(2,1)S(1)} %get-tuple-element.45), channel_id=1, source_target_pairs={{0,8},{8,0},{16,24},{24,16},{1,9},{9,1},{17,25},{25,17},{2,10},{10... | collective-permute-start | bytes 245768 | tf_op jit(solution)/shard_map/ppermute | solution.py:361
  97.6 7.4 %collective-permute-start.25 = (bf16[32,1280]{1,0:T(8,128)(2,1)S(1)}, bf16[32,1280]{1,0:T(8,128)(2,1)S(1)}, u32[]{:S(2)}, u32[]{:S(2)}) collective-permute-start(bf16[32,1280]{1,0:T(8,128)(2,1)S(1)} %get-tuple-element.46), channel_id=1, source_target_pairs={{0,16},{8,24},{16,0},{24,8},{1,17},{9,25},{17,1},{25,9},{2,18},{10... | collective-permute-start | bytes 245768 | tf_op jit(solution)/shard_map/ppermute | solution.py:361
  98.8 6.3 %collective-permute-start.26 = (bf16[32,1280]{1,0:T(8,128)(2,1)S(1)}, bf16[32,1280]{1,0:T(8,128)(2,1)S(1)}, u32[]{:S(2)}, u32[]{:S(2)}) collective-permute-start(bf16[32,1280]{1,0:T(8,128)(2,1)S(1)} %get-tuple-element.47), channel_id=1, source_target_pairs={{0,24},{8,16},{16,8},{24,0},{1,25},{9,17},{17,9},{25,1},{2,26},{10... | collective-permute-start | bytes 245768 | tf_op jit(solution)/shard_map/ppermute | solution.py:361
  (7 other events, 105.3 us)
where the time goes:
time: 106 us
  starting transfers between devices  39.9 us (38%)
  waiting for transfers between devices  38.4 us (36%)
  Pallas kernels  24.5 us (23%)
  local copies, waits for them, and re-layouts  2.28 us (2%)
    ppermute x33, starting transfers between devices, over(): return lax.ppermute(value, axis, [(i, i ^ mask) for i in range(size)])  39.9 us
    ppermute x33, waiting for transfers between devices, over(): return lax.ppermute(value, axis, [(i, i ^ mask) for i in range(size)])  38.4 us
    pallas_call x2, Pallas kernels, attend(): pl.pallas_call(kernel, out_shape=[jax.ShapeDtypeStruct((row_count, width)...  17 us
    pallas_call x1, Pallas kernels, project(): pl.pallas_call(kernel, out_shape=jax.ShapeDtypeStruct((row_count, out_wid...  2.93 us
    pallas_call x1, Pallas kernels, weight_gradient(): pl.pallas_call(kernel, out_shape=[shape(chips * group, out_width - split,...  2.84 us
    unnamed x12, local copies, waits for them, and re-layouts  2.28 us
  transfers between devices with their start and end apart: 33, of which 7 were waited for; matrix products, arithmetic and copies ran while one was open for 0% of the time, Pallas kernels for 19%

commit v1 on v0

--- a/solution.py
+++ b/solution.py
@@ -60,7 +60,7 @@
         scratch_shapes=[pltpu.SemaphoreType.DMA((count * chips,))],
         compiler_params=params(16),
         name="cut",
-    )(*sources)
+    )(*(pltpu.with_memory_space_constraint(source, pltpu.HBM) for source in sources))
 
 
 def assemble(near, far, chips):
@@ -90,7 +90,7 @@
     total = both.shape[0]
     heads = width // HEAD
     count = len(queries)
-    choices = 4
+    choices = 3
     step_k = total // choices
     scale = float(HEAD) ** -0.5 * LOG2E
 
@@ -377,7 +377,7 @@
     grad_far = other_core(grad_near)
     both = assemble(near, far, chips)
     mine = [None] * chips
-    for aways in (list(range(chips - 1)), [chips - 1]):
+    for aways in ([chips - 1], list(range(1, chips - 1)), [0]):
         results = attend([queries[i] for i in aways], [ends[i] for i in aways], aways, both, width)
         for away, piece in zip(aways, results):
             mine[away] = over("seq", seq, piece, 2 * away) if away else piece

time: 106 us -> 103 us (0.972)
  Pallas kernels: 24.5 us -> 27.9 us
  starting transfers between devices: 39.9 us -> 37 us
  local copies, waits for them, and re-layouts: 2.28 us -> 0.01 us
  waiting for transfers between devices: 38.4 us -> 36.8 us
    ppermute x33, starting transfers between devices: 39.9 us -> 37 us  [over(): return lax.ppermute(value, axis, [(i, i ^ mask) for i in range(size)])]
    pallas_call x2, Pallas kernels: 0.45 us -> 2.92 us  [cut(): pl.pallas_call(kernel, out_shape=[shape] * chips, in_specs=[HBM] * count,...]
    unnamed x12 -> x6, local copies, waits for them, and re-layouts: 2.28 us -> 0.01 us
    ppermute x33, waiting for transfers between devices: 38.4 us -> 36.8 us  [over(): return lax.ppermute(value, axis, [(i, i ^ mask) for i in range(size)])]
    pallas_call x2 -> x3, Pallas kernels: 17 us -> 18 us  [attend(): pl.pallas_call(kernel, out_shape=[jax.ShapeDtypeStruct((row_count, width)...]
  transfers between devices with their start and end apart: 33 -> 33, of which waited for: 7 -> 8; matrix products, arithmetic and copies ran while one was open for 0% -> 0% of each run, Pallas kernels for 19% -> 22%
where the time goes in v1:
time: 103 us; the launch traced here: 102 us
  starting transfers between devices  37 us (36%)
  waiting for transfers between devices  36.8 us (36%)
  Pallas kernels  27.9 us (27%)
    ppermute x33, starting transfers between devices, over(): return lax.ppermute(value, axis, [(i, i ^ mask) for i in range(size)])  37 us
    ppermute x33, waiting for transfers between devices, over(): return lax.ppermute(value, axis, [(i, i ^ mask) for i in range(size)])  36.8 us
    pallas_call x3, Pallas kernels, attend(): pl.pallas_call(kernel, out_shape=[jax.ShapeDtypeStruct((row_count, width)...  18 us
    pallas_call x1, Pallas kernels, project(): pl.pallas_call(kernel, out_shape=jax.ShapeDtypeStruct((row_count, out_wid...  2.93 us
    pallas_call x2, Pallas kernels, cut(): pl.pallas_call(kernel, out_shape=[shape] * chips, in_specs=[HBM] * count,...  2.92 us
    pallas_call x1, Pallas kernels, weight_gradient(): pl.pallas_call(kernel, out_shape=[shape(chips * group, out_width - split,...  2.81 us
  transfers between devices with their start and end apart: 33, of which 8 were waited for; matrix products, arithmetic and copies ran while one was open for 0% of the time, Pallas kernels for 22%

profile of v1, /device:TPU:0, one launch (start us, length us, event | category | flops | bytes accessed | tf_op | source)
XLA Modules:
  0.0 102.4 jit_solution(6985856931941498817)
XLA Ops:
  0.7 1.7 %cut.3 = (bf16[384,512]{1,0:T(8,128)(2,1)S(1)}, bf16[384,512]{1,0:T(8,128)(2,1)S(1)}, bf16[384,512]{1,0:T(8,128)(2,1)S(1)}, bf16[384,512]{1,0:T(8,128)(2,1)S(1)}) custom-call(bf16[384,1024]{1,0:T(8,128)(2,1)} %bitcast.8, bf16[384,1024]{1,0:T(8,128)(2,1)} %bitcast.9), custom_call_target="tpu_custom_call" | custom-call | tf_op jit(solution)/shard_map/cut/pallas_call | solution.py:55
  2.3 3.0 %collective-permute-start = (bf16[384,512]{1,0:T(8,128)(2,1)S(1)}, bf16[384,512]{1,0:T(8,128)(2,1)S(1)}, u32[]{:S(2)}, u32[]{:S(2)}) collective-permute-start(bf16[384,512]{1,0:T(8,128)(2,1)S(1)} %get-tuple-element.30), channel_id=1, source_target_pairs={{0,2},{1,3},{2,0},{3,1},{4,6},{5,7},{6,4},{7,5},{8,10},{9,11},{10,... | collective-permute-start | bytes 1179656 | tf_op jit(solution)/shard_map/ppermute | solution.py:361
  5.4 1.5 %collective-permute-start.1 = (bf16[384,512]{1,0:T(8,128)(2,1)S(1)}, bf16[384,512]{1,0:T(8,128)(2,1)S(1)}, u32[]{:S(2)}, u32[]{:S(2)}) collective-permute-start(bf16[384,512]{1,0:T(8,128)(2,1)S(1)} %get-tuple-element.31), channel_id=1, source_target_pairs={{0,4},{1,5},{2,6},{3,7},{4,0},{5,1},{6,2},{7,3},{8,12},{9,13},{10,... | collective-permute-start | bytes 1179656 | tf_op jit(solution)/shard_map/ppermute | solution.py:361
  7.1 8.2 %collective-permute-done.refs_1_ = bf16[384,512]{1,0:T(8,128)(2,1)S(1)} collective-permute-done((bf16[384,512]{1,0:T(8,128)(2,1)S(1)}, bf16[384,512]{1,0:T(8,128)(2,1)S(1)}, u32[]{:S(2)}, u32[]{:S(2)}) %collective-permute-start) | collective-permute-done | bytes 393248 | tf_op jit(solution)/shard_map/ppermute | solution.py:361
  15.3 10.0 %collective-permute-done.1.refs_2_ = bf16[384,512]{1,0:T(8,128)(2,1)S(1)} collective-permute-done((bf16[384,512]{1,0:T(8,128)(2,1)S(1)}, bf16[384,512]{1,0:T(8,128)(2,1)S(1)}, u32[]{:S(2)}, u32[]{:S(2)}) %collective-permute-start.1) | collective-permute-done | bytes 393248 | tf_op jit(solution)/shard_map/ppermute | solution.py:361
  25.8 1.3 %cut.2 = (bf16[384,256]{1,0:T(8,128)(2,1)S(1)}, bf16[384,256]{1,0:T(8,128)(2,1)S(1)}, bf16[384,256]{1,0:T(8,128)(2,1)S(1)}, bf16[384,256]{1,0:T(8,128)(2,1)S(1)}) custom-call(bf16[384,1024]{1,0:T(8,128)(2,1)} %bitcast.10), custom_call_target="tpu_custom_call" | custom-call | tf_op jit(solution)/shard_map/cut/pallas_call | solution.py:55
  27.1 1.6 %collective-permute-start.10 = (bf16[384,256]{1,0:T(8,128)(2,1)S(1)}, bf16[384,256]{1,0:T(8,128)(2,1)S(1)}, u32[]{:S(2)}, u32[]{:S(2)}) collective-permute-start(bf16[384,256]{1,0:T(8,128)(2,1)S(1)} %get-tuple-element.34), channel_id=1, source_target_pairs={{0,4},{1,5},{2,6},{3,7},{4,0},{5,1},{6,2},{7,3},{8,12},{9,13},{10,... | collective-permute-start | bytes 589832 | tf_op jit(solution)/shard_map/ppermute | solution.py:361
  29.2 1.5 %collective-permute-start.7 = (s32[384]{0:T(512)S(1)}, s32[384]{0:T(512)S(1)}, u32[]{:S(2)}, u32[]{:S(2)}) collective-permute-start(s32[384]{0:T(512)S(1)} %copy-done.2), channel_id=1, source_target_pairs={{0,2},{1,3},{2,0},{3,1},{4,6},{5,7},{6,4},{7,5},{8,10},{9,11},{10,... | collective-permute-start | bytes 4616 | tf_op jit(solution)/shard_map/ppermute | solution.py:361
  31.5 3.8 %collective-permute-done.7.refs_0_ = s32[384]{0:T(512)S(1)} collective-permute-done((s32[384]{0:T(512)S(1)}, s32[384]{0:T(512)S(1)}, u32[]{:S(2)}, u32[]{:S(2)}) %collective-permute-start.7) | collective-permute-done | bytes 1568 | tf_op jit(solution)/shard_map/ppermute | solution.py:361
  35.6 2.6 %collective-permute-start.14 = (bf16[384,256]{1,0:T(8,128)(2,1)S(1)}, bf16[384,256]{1,0:T(8,128)(2,1)S(1)}, u32[]{:S(2)}, u32[]{:S(2)}) collective-permute-start(bf16[384,256]{1,0:T(8,128)(2,1)S(1)} %get-tuple-element.37), channel_id=1, source_target_pairs={{0,6},{1,7},{2,4},{3,5},{4,2},{5,3},{6,0},{7,1},{8,14},{9,15},{10,... | collective-permute-start | bytes 589832 | tf_op jit(solution)/shard_map/ppermute | solution.py:361
  38.2 9.3 %attend.4 = (bf16[384,256]{1,0:T(8,128)(2,1)S(1)}, bf16[384,256]{1,0:T(8,128)(2,1)S(1)}) custom-call(s32[384]{0:T(512)S(1)} %collective-permute-done.7.refs_0_, s32[384]{0:T(512)S(1)} %collective-permute-done.8.refs_1_, bf16[384,256]{1,0:T(8,128)(2,1)S(1)} %collective-permute-done.9.refs_2_, bf16[384,256]{1,0:T(8,128)(2,1)S(1)} %collective-permute-done.10.refs_3_, ...), custom_call_target="tpu_custom_call" | custom-call | flops 2415919104 | bytes 3145728 | tf_op jit(solution)/shard_map/attend/pallas_call | solution.py:178
  47.5 0.9 collective-permute-start.12
  48.4 5.1 %attend.5 = bf16[384,256]{1,0:T(8,128)(2,1)S(1)} custom-call(s32[384]{0:T(512)S(1)} %collective-permute-done.13.refs_0_, bf16[384,256]{1,0:T(8,128)(2,1)S(1)} %collective-permute-done.14.refs_1_, bf16[3072,512]{1,0:T(8,128)(2,1)S(1)} %assemble.1.refs_2_.refs_4_), custom_call_target="tpu_custom_call" | custom-call | flops 1207959552 | bytes 3145728 | tf_op jit(solution)/shard_map/attend/pallas_call | solution.py:178
  53.6 1.1 %collective-permute-start.15 = (bf16[384,256]{1,0:T(8,128)(2,1)S(1)}, bf16[384,256]{1,0:T(8,128)(2,1)S(1)}, u32[]{:S(2)}, u32[]{:S(2)}) collective-permute-start(bf16[384,256]{1,0:T(8,128)(2,1)S(1)} %attend.5), channel_id=1, source_target_pairs={{0,6},{1,7},{2,4},{3,5},{4,2},{5,3},{6,0},{7,1},{8,14},{9,15},{10,... | collective-permute-start | bytes 589832 | tf_op jit(solution)/shard_map/ppermute | solution.py:361
  54.7 3.7 %attend.3.refs_0_ = bf16[384,256]{1,0:T(8,128)(2,1)S(1)} custom-call(s32[384]{0:T(512)S(1)} %copy-done.2, bf16[384,256]{1,0:T(8,128)(2,1)S(1)} %get-tuple-element.28.refs_1_, bf16[3072,512]{1,0:T(8,128)(2,1)S(1)} %assemble.1.refs_2_.refs_4_), custom_call_target="tpu_custom_call" | custom-call | flops 1207959552 | bytes 3145728 | tf_op jit(solution)/shard_map/attend/pallas_call | solution.py:178
  59.1 1.1 %collective-permute-done.15.refs_3_ = bf16[384,256]{1,0:T(8,128)(2,1)S(1)} collective-permute-done((bf16[384,256]{1,0:T(8,128)(2,1)S(1)}, bf16[384,256]{1,0:T(8,128)(2,1)S(1)}, u32[]{:S(2)}, u32[]{:S(2)}) %collective-permute-start.15) | collective-permute-done | bytes 196640 | tf_op jit(solution)/shard_map/ppermute | solution.py:361
  60.5 1.2 %collective-permute-done.19.refs_7_ = bf16[384,256]{1,0:T(8,128)(2,1)S(1)} collective-permute-done((bf16[384,256]{1,0:T(8,128)(2,1)S(1)}, bf16[384,256]{1,0:T(8,128)(2,1)S(1)}, u32[]{:S(2)}, u32[]{:S(2)}) %collective-permute-start.19) | collective-permute-done | bytes 196640 | tf_op jit(solution)/shard_map/ppermute | solution.py:361
  61.7 2.8 %weight_gradient.1 = (f32[128,768]{1,0:T(8,128)S(1)}, bf16[128,768]{1,0:T(8,128)(2,1)S(1)}, bf16[128,768]{1,0:T(8,128)(2,1)S(1)}, bf16[128,768]{1,0:T(8,128)(2,1...) custom-call(bf16[384,256]{1,0:T(8,128)(2,1)S(1)} %attend.3.refs_0_, ...), custom_call_target="tpu_custom_call" | custom-call | flops 1610612736 | bytes 3145728 | tf_op jit(solution)/shard_map/weight_gradient/pallas_call | solution.py:246
  64.5 1.8 %collective-permute-start.27 = (bf16[128,768]{1,0:T(8,128)(2,1)S(1)}, bf16[128,768]{1,0:T(8,128)(2,1)S(1)}, u32[]{:S(2)}, u32[]{:S(2)}) collective-permute-start(bf16[128,768]{1,0:T(8,128)(2,1)S(1)} %get-tuple-element.47), channel_id=1, source_target_pairs={{0,8},{8,0},{16,24},{24,16},{1,9},{9,1},{17,25},{25,17},{2,10},{10... | collective-permute-start | bytes 589832 | tf_op jit(solution)/shard_map/ppermute | solution.py:361
  66.3 2.0 %collective-permute-start.21 = (bf16[128,1280]{1,0:T(8,128)(2,1)S(1)}, bf16[128,1280]{1,0:T(8,128)(2,1)S(1)}, u32[]{:S(2)}, u32[]{:S(2)}) collective-permute-start(bf16[128,1280]{1,0:T(8,128)(2,1)S(1)} %get-tuple-element.39), channel_id=1, source_target_pairs={{0,2},{1,3},{2,0},{3,1},{4,6},{5,7},{6,4},{7,5},{8,10},{9,11},{10,... | collective-permute-start | bytes 983048 | tf_op jit(solution)/shard_map/ppermute | solution.py:361
  68.3 1.0 collective-permute-start.22
  69.8 2.6 %collective-permute-start.28 = (bf16[128,768]{1,0:T(8,128)(2,1)S(1)}, bf16[128,768]{1,0:T(8,128)(2,1)S(1)}, u32[]{:S(2)}, u32[]{:S(2)}) collective-permute-start(bf16[128,768]{1,0:T(8,128)(2,1)S(1)} %get-tuple-element.48), channel_id=1, source_target_pairs={{0,16},{8,24},{16,0},{24,8},{1,17},{9,25},{17,1},{25,9},{2,18},{10... | collective-permute-start | bytes 589832 | tf_op jit(solution)/shard_map/ppermute | solution.py:361
  72.4 3.9 %collective-permute-start.29 = (bf16[128,768]{1,0:T(8,128)(2,1)S(1)}, bf16[128,768]{1,0:T(8,128)(2,1)S(1)}, u32[]{:S(2)}, u32[]{:S(2)}) collective-permute-start(bf16[128,768]{1,0:T(8,128)(2,1)S(1)} %get-tuple-element.49), channel_id=1, source_target_pairs={{0,24},{8,16},{16,8},{24,0},{1,25},{9,17},{17,9},{25,1},{2,26},{10... | collective-permute-start | bytes 589832 | tf_op jit(solution)/shard_map/ppermute | solution.py:361
  76.3 9.9 %collective-permute-done.28.refs_2_ = bf16[128,768]{1,0:T(8,128)(2,1)S(1)} collective-permute-done((bf16[128,768]{1,0:T(8,128)(2,1)S(1)}, bf16[128,768]{1,0:T(8,128)(2,1)S(1)}, u32[]{:S(2)}, u32[]{:S(2)}) %collective-permute-start.28) | collective-permute-done | bytes 196640 | tf_op jit(solution)/shard_map/ppermute | solution.py:361
  86.3 2.2 %collective-permute-start.30 = (bf16[32,768]{1,0:T(8,128)(2,1)S(1)}, bf16[32,768]{1,0:T(8,128)(2,1)S(1)}, u32[]{:S(2)}, u32[]{:S(2)}) collective-permute-start(bf16[32,768]{1,0:T(8,128)(2,1)S(1)} %get-tuple-element.51), channel_id=1, source_target_pairs={{0,2},{1,3},{2,0},{3,1},{4,6},{5,7},{6,4},{7,5},{8,10},{9,11},{10,... | collective-permute-start | bytes 147464 | tf_op jit(solution)/shard_map/ppermute | solution.py:361
  88.4 1.0 collective-permute-start.31
  90.1 3.8 %collective-permute-start.24 = (bf16[32,1280]{1,0:T(8,128)(2,1)S(1)}, bf16[32,1280]{1,0:T(8,128)(2,1)S(1)}, u32[]{:S(2)}, u32[]{:S(2)}) collective-permute-start(bf16[32,1280]{1,0:T(8,128)(2,1)S(1)} %get-tuple-element.43), channel_id=1, source_target_pairs={{0,8},{8,0},{16,24},{24,16},{1,9},{9,1},{17,25},{25,17},{2,10},{10... | collective-permute-start | bytes 245768 | tf_op jit(solution)/shard_map/ppermute | solution.py:361
  93.9 1.1 %collective-permute-start.25 = (bf16[32,1280]{1,0:T(8,128)(2,1)S(1)}, bf16[32,1280]{1,0:T(8,128)(2,1)S(1)}, u32[]{:S(2)}, u32[]{:S(2)}) collective-permute-start(bf16[32,1280]{1,0:T(8,128)(2,1)S(1)} %get-tuple-element.44), channel_id=1, source_target_pairs={{0,16},{8,24},{16,0},{24,8},{1,17},{9,25},{17,1},{25,9},{2,18},{10... | collective-permute-start | bytes 245768 | tf_op jit(solution)/shard_map/ppermute | solution.py:361
  95.1 1.4 %collective-permute-start.26 = (bf16[32,1280]{1,0:T(8,128)(2,1)S(1)}, bf16[32,1280]{1,0:T(8,128)(2,1)S(1)}, u32[]{:S(2)}, u32[]{:S(2)}) collective-permute-start(bf16[32,1280]{1,0:T(8,128)(2,1)S(1)} %get-tuple-element.45), channel_id=1, source_target_pairs={{0,24},{8,16},{16,8},{24,0},{1,25},{9,17},{17,9},{25,1},{2,26},{10... | collective-permute-start | bytes 245768 | tf_op jit(solution)/shard_map/ppermute | solution.py:361
  96.5 2.9 %project.1 = bf16[384,2048]{1,0:T(8,128)(2,1)} custom-call(bf16[384,256]{1,0:T(8,128)(2,1)S(1)} %attend.3.refs_0_, bf16[384,256]{1,0:T(8,128)(2,1)S(1)} %collective-permute-done.11.refs_1_, bf16[384,256]{1,0:T(8,128)(2,1)S(1)} %collective-permute-done.12.refs_2_, bf16[384,256]{1,0:T(8,128)(2,1)S(1)} %collective-permute-done.15.refs_3_, ...), custom_call_target="tpu_custom_call" | custom-call | flops 1610612736 | bytes 4194304 | tf_op jit(solution)/shard_map/project/pallas_call | solution.py:287
  99.4 2.3 %collective-permute-done.25.refs_2_ = bf16[32,1280]{1,0:T(8,128)(2,1)S(1)} collective-permute-done((bf16[32,1280]{1,0:T(8,128)(2,1)S(1)}, bf16[32,1280]{1,0:T(8,128)(2,1)S(1)}, u32[]{:S(2)}, u32[]{:S(2)}) %collective-permute-start.25) | collective-permute-done | bytes 81952 | tf_op jit(solution)/shard_map/ppermute | solution.py:361
  101.7 0.8 finish.1
  (51 shorter events, 4.7 us)
Async XLA Ops:
  2.3 13.0 %collective-permute-start = (bf16[384,512]{1,0:T(8,128)(2,1)S(1)}, bf16[384,512]{1,0:T(8,128)(2,1)S(1)}, u32[]{:S(2)}, u32[]{:S(2)}) collective-permute-start(bf16[384,512]{1,0:T(8,128)(2,1)S(1)} %get-tuple-element.30), channel_id=1, source_target_pairs={{0,2},{1,3},{2,0},{3,1},{4,6},{5,7},{6,4},{7,5},{8,10},{9,11},{10,... | collective-permute-start | bytes 1179656 | tf_op jit(solution)/shard_map/ppermute | solution.py:361
  5.4 56.3 %collective-permute-start.20 = (bf16[384,2048]{1,0:T(8,128)(2,1)S(1)}, bf16[384,2048]{1,0:T(8,128)(2,1)S(1)}, u32[]{:S(2)}, u32[]{:S(2)}) collective-permute-start(bf16[384,2048]{1,0:T(8,128)(2,1)S(1)} %bitcast.5), channel_id=1, source_target_pairs={{0,1},{1,0},{2,3},{3,2},{4,5},{5,4},{6,7},{7,6},{8,9},{9,8},{10,11... | collective-permute-start | bytes 4718600 | tf_op jit(solution)/shard_map/ppermute | solution.py:361
  5.4 20.0 %collective-permute-start.1 = (bf16[384,512]{1,0:T(8,128)(2,1)S(1)}, bf16[384,512]{1,0:T(8,128)(2,1)S(1)}, u32[]{:S(2)}, u32[]{:S(2)}) collective-permute-start(bf16[384,512]{1,0:T(8,128)(2,1)S(1)} %get-tuple-element.31), channel_id=1, source_target_pairs={{0,4},{1,5},{2,6},{3,7},{4,0},{5,1},{6,2},{7,3},{8,12},{9,13},{10,... | collective-permute-start | bytes 1179656 | tf_op jit(solution)/shard_map/ppermute | solution.py:361
  6.9 18.4 %collective-permute-start.2 = (bf16[384,512]{1,0:T(8,128)(2,1)S(1)}, bf16[384,512]{1,0:T(8,128)(2,1)S(1)}, u32[]{:S(2)}, u32[]{:S(2)}) collective-permute-start(bf16[384,512]{1,0:T(8,128)(2,1)S(1)} %get-tuple-element.32), channel_id=1, source_target_pairs={{0,6},{1,7},{2,4},{3,5},{4,2},{5,3},{6,0},{7,1},{8,14},{9,15},{10,... | collective-permute-start | bytes 1179656 | tf_op jit(solution)/shard_map/ppermute | solution.py:361
  7.1 20.0 %collective-permute-start.3 = (bf16[384,512]{1,0:T(8,128)(2,1)S(1)}, bf16[384,512]{1,0:T(8,128)(2,1)S(1)}, u32[]{:S(2)}, u32[]{:S(2)}) collective-permute-start(bf16[384,512]{1,0:T(8,128)(2,1)S(1)} %get-tuple-element.29.refs_0_), channel_id=1, source_target_pairs={{0,1},{1,0},{2,3},{3,2},{4,5},{5,4},{6,7},{7,6},{8,9},{9,8},{10,11... | collective-permute-start | bytes 1179656 | tf_op jit(solution)/shard_map/ppermute | solution.py:361
  15.3 13.4 %collective-permute-start.4 = (bf16[384,512]{1,0:T(8,128)(2,1)S(1)}, bf16[384,512]{1,0:T(8,128)(2,1)S(1)}, u32[]{:S(2)}, u32[]{:S(2)}) collective-permute-start(bf16[384,512]{1,0:T(8,128)(2,1)S(1)} %collective-permute-done.refs_1_), channel_id=1, source_target_pairs={{0,1},{1,0},{2,3},{3,2},{4,5},{5,4},{6,7},{7,6},{8,9},{9,8},{10,11... | collective-permute-start | bytes 1179656 | tf_op jit(solution)/shard_map/ppermute | solution.py:361
  25.3 3.9 %collective-permute-start.5 = (bf16[384,512]{1,0:T(8,128)(2,1)S(1)}, bf16[384,512]{1,0:T(8,128)(2,1)S(1)}, u32[]{:S(2)}, u32[]{:S(2)}) collective-permute-start(bf16[384,512]{1,0:T(8,128)(2,1)S(1)} %collective-permute-done.1.refs_2_), channel_id=1, source_target_pairs={{0,1},{1,0},{2,3},{3,2},{4,5},{5,4},{6,7},{7,6},{8,9},{9,8},{10,11... | collective-permute-start | bytes 1179656 | tf_op jit(solution)/shard_map/ppermute | solution.py:361
  25.3 5.4 %collective-permute-start.6 = (bf16[384,512]{1,0:T(8,128)(2,1)S(1)}, bf16[384,512]{1,0:T(8,128)(2,1)S(1)}, u32[]{:S(2)}, u32[]{:S(2)}) collective-permute-start(bf16[384,512]{1,0:T(8,128)(2,1)S(1)} %collective-permute-done.2.refs_3_), channel_id=1, source_target_pairs={{0,1},{1,0},{2,3},{3,2},{4,5},{5,4},{6,7},{7,6},{8,9},{9,8},{10,11... | collective-permute-start | bytes 1179656 | tf_op jit(solution)/shard_map/ppermute | solution.py:361
  27.1 11.1 %collective-permute-start.10 = (bf16[384,256]{1,0:T(8,128)(2,1)S(1)}, bf16[384,256]{1,0:T(8,128)(2,1)S(1)}, u32[]{:S(2)}, u32[]{:S(2)}) collective-permute-start(bf16[384,256]{1,0:T(8,128)(2,1)S(1)} %get-tuple-element.34), channel_id=1, source_target_pairs={{0,4},{1,5},{2,6},{3,7},{4,0},{5,1},{6,2},{7,3},{8,12},{9,13},{10,... | collective-permute-start | bytes 589832 | tf_op jit(solution)/shard_map/ppermute | solution.py:361
  28.7 9.5 %collective-permute-start.9 = (bf16[384,256]{1,0:T(8,128)(2,1)S(1)}, bf16[384,256]{1,0:T(8,128)(2,1)S(1)}, u32[]{:S(2)}, u32[]{:S(2)}) collective-permute-start(bf16[384,256]{1,0:T(8,128)(2,1)S(1)} %get-tuple-element.33), channel_id=1, source_target_pairs={{0,2},{1,3},{2,0},{3,1},{4,6},{5,7},{6,4},{7,5},{8,10},{9,11},{10,... | collective-permute-start | bytes 589832 | tf_op jit(solution)/shard_map/ppermute | solution.py:361
  29.2 6.0 %collective-permute-start.7 = (s32[384]{0:T(512)S(1)}, s32[384]{0:T(512)S(1)}, u32[]{:S(2)}, u32[]{:S(2)}) collective-permute-start(s32[384]{0:T(512)S(1)} %copy-done.2), channel_id=1, source_target_pairs={{0,2},{1,3},{2,0},{3,1},{4,6},{5,7},{6,4},{7,5},{8,10},{9,11},{10,... | collective-permute-start | bytes 4616 | tf_op jit(solution)/shard_map/ppermute | solution.py:361
  30.7 4.9 %collective-permute-start.8 = (s32[384]{0:T(512)S(1)}, s32[384]{0:T(512)S(1)}, u32[]{:S(2)}, u32[]{:S(2)}) collective-permute-start(s32[384]{0:T(512)S(1)} %copy-done.2), channel_id=1, source_target_pairs={{0,4},{1,5},{2,6},{3,7},{4,0},{5,1},{6,2},{7,3},{8,12},{9,13},{10,... | collective-permute-start | bytes 4616 | tf_op jit(solution)/shard_map/ppermute | solution.py:361
  35.3 13.2 %collective-permute-start.13 = (s32[384]{0:T(512)S(1)}, s32[384]{0:T(512)S(1)}, u32[]{:S(2)}, u32[]{:S(2)}) collective-permute-start(s32[384]{0:T(512)S(1)} %copy-done.2), channel_id=1, source_target_pairs={{0,6},{1,7},{2,4},{3,5},{4,2},{5,3},{6,0},{7,1},{8,14},{9,15},{10,... | collective-permute-start | bytes 4616 | tf_op jit(solution)/shard_map/ppermute | solution.py:361
  35.6 12.8 %collective-permute-start.14 = (bf16[384,256]{1,0:T(8,128)(2,1)S(1)}, bf16[384,256]{1,0:T(8,128)(2,1)S(1)}, u32[]{:S(2)}, u32[]{:S(2)}) collective-permute-start(bf16[384,256]{1,0:T(8,128)(2,1)S(1)} %get-tuple-element.37), channel_id=1, source_target_pairs={{0,6},{1,7},{2,4},{3,5},{4,2},{5,3},{6,0},{7,1},{8,14},{9,15},{10,... | collective-permute-start | bytes 589832 | tf_op jit(solution)/shard_map/ppermute | solution.py:361
  47.5 11.0 %collective-permute-start.11 = (bf16[384,256]{1,0:T(8,128)(2,1)S(1)}, bf16[384,256]{1,0:T(8,128)(2,1)S(1)}, u32[]{:S(2)}, u32[]{:S(2)}) collective-permute-start(bf16[384,256]{1,0:T(8,128)(2,1)S(1)} %get-tuple-element.35), channel_id=1, source_target_pairs={{0,2},{1,3},{2,0},{3,1},{4,6},{5,7},{6,4},{7,5},{8,10},{9,11},{10,... | collective-permute-start | bytes 589832 | tf_op jit(solution)/shard_map/ppermute | solution.py:361
  47.5 11.4 %collective-permute-start.12 = (bf16[384,256]{1,0:T(8,128)(2,1)S(1)}, bf16[384,256]{1,0:T(8,128)(2,1)S(1)}, u32[]{:S(2)}, u32[]{:S(2)}) collective-permute-start(bf16[384,256]{1,0:T(8,128)(2,1)S(1)} %get-tuple-element.36), channel_id=1, source_target_pairs={{0,4},{1,5},{2,6},{3,7},{4,0},{5,1},{6,2},{7,3},{8,12},{9,13},{10,... | collective-permute-start | bytes 589832 | tf_op jit(solution)/shard_map/ppermute | solution.py:361
  53.6 6.6 %collective-permute-start.15 = (bf16[384,256]{1,0:T(8,128)(2,1)S(1)}, bf16[384,256]{1,0:T(8,128)(2,1)S(1)}, u32[]{:S(2)}, u32[]{:S(2)}) collective-permute-start(bf16[384,256]{1,0:T(8,128)(2,1)S(1)} %attend.5), channel_id=1, source_target_pairs={{0,6},{1,7},{2,4},{3,5},{4,2},{5,3},{6,0},{7,1},{8,14},{9,15},{10,... | collective-permute-start | bytes 589832 | tf_op jit(solution)/shard_map/ppermute | solution.py:361
  58.4 1.8 %collective-permute-start.16 = (bf16[384,256]{1,0:T(8,128)(2,1)S(1)}, bf16[384,256]{1,0:T(8,128)(2,1)S(1)}, u32[]{:S(2)}, u32[]{:S(2)}) collective-permute-start(bf16[384,256]{1,0:T(8,128)(2,1)S(1)} %attend.3.refs_0_), channel_id=1, source_target_pairs={{0,1},{1,0},{2,3},{3,2},{4,5},{5,4},{6,7},{7,6},{8,9},{9,8},{10,11... | collective-permute-start | bytes 589832 | tf_op jit(solution)/shard_map/ppermute | solution.py:361
  58.5 1.7 %collective-permute-start.17 = (bf16[384,256]{1,0:T(8,128)(2,1)S(1)}, bf16[384,256]{1,0:T(8,128)(2,1)S(1)}, u32[]{:S(2)}, u32[]{:S(2)}) collective-permute-start(bf16[384,256]{1,0:T(8,128)(2,1)S(1)} %collective-permute-done.11.refs_1_), channel_id=1, source_target_pairs={{0,1},{1,0},{2,3},{3,2},{4,5},{5,4},{6,7},{7,6},{8,9},{9,8},{10,11... | collective-permute-start | bytes 589832 | tf_op jit(solution)/shard_map/ppermute | solution.py:361
  59.0 1.5 %collective-permute-start.18 = (bf16[384,256]{1,0:T(8,128)(2,1)S(1)}, bf16[384,256]{1,0:T(8,128)(2,1)S(1)}, u32[]{:S(2)}, u32[]{:S(2)}) collective-permute-start(bf16[384,256]{1,0:T(8,128)(2,1)S(1)} %collective-permute-done.12.refs_2_), channel_id=1, source_target_pairs={{0,1},{1,0},{2,3},{3,2},{4,5},{5,4},{6,7},{7,6},{8,9},{9,8},{10,11... | collective-permute-start | bytes 589832 | tf_op jit(solution)/shard_map/ppermute | solution.py:361
  64.5 7.9 %collective-permute-start.27 = (bf16[128,768]{1,0:T(8,128)(2,1)S(1)}, bf16[128,768]{1,0:T(8,128)(2,1)S(1)}, u32[]{:S(2)}, u32[]{:S(2)}) collective-permute-start(bf16[128,768]{1,0:T(8,128)(2,1)S(1)} %get-tuple-element.47), channel_id=1, source_target_pairs={{0,8},{8,0},{16,24},{24,16},{1,9},{9,1},{17,25},{25,17},{2,10},{10... | collective-permute-start | bytes 589832 | tf_op jit(solution)/shard_map/ppermute | solution.py:361
  66.3 23.1 %collective-permute-start.21 = (bf16[128,1280]{1,0:T(8,128)(2,1)S(1)}, bf16[128,1280]{1,0:T(8,128)(2,1)S(1)}, u32[]{:S(2)}, u32[]{:S(2)}) collective-permute-start(bf16[128,1280]{1,0:T(8,128)(2,1)S(1)} %get-tuple-element.39), channel_id=1, source_target_pairs={{0,2},{1,3},{2,0},{3,1},{4,6},{5,7},{6,4},{7,5},{8,10},{9,11},{10,... | collective-permute-start | bytes 983048 | tf_op jit(solution)/shard_map/ppermute | solution.py:361
  68.3 21.7 %collective-permute-start.22 = (bf16[128,1280]{1,0:T(8,128)(2,1)S(1)}, bf16[128,1280]{1,0:T(8,128)(2,1)S(1)}, u32[]{:S(2)}, u32[]{:S(2)}) collective-permute-start(bf16[128,1280]{1,0:T(8,128)(2,1)S(1)} %get-tuple-element.40), channel_id=1, source_target_pairs={{0,4},{1,5},{2,6},{3,7},{4,0},{5,1},{6,2},{7,3},{8,12},{9,13},{10,... | collective-permute-start | bytes 983048 | tf_op jit(solution)/shard_map/ppermute | solution.py:361
  69.3 20.7 %collective-permute-start.23 = (bf16[128,1280]{1,0:T(8,128)(2,1)S(1)}, bf16[128,1280]{1,0:T(8,128)(2,1)S(1)}, u32[]{:S(2)}, u32[]{:S(2)}) collective-permute-start(bf16[128,1280]{1,0:T(8,128)(2,1)S(1)} %get-tuple-element.41), channel_id=1, source_target_pairs={{0,6},{1,7},{2,4},{3,5},{4,2},{5,3},{6,0},{7,1},{8,14},{9,15},{10,... | collective-permute-start | bytes 983048 | tf_op jit(solution)/shard_map/ppermute | solution.py:361
  69.8 16.4 %collective-permute-start.28 = (bf16[128,768]{1,0:T(8,128)(2,1)S(1)}, bf16[128,768]{1,0:T(8,128)(2,1)S(1)}, u32[]{:S(2)}, u32[]{:S(2)}) collective-permute-start(bf16[128,768]{1,0:T(8,128)(2,1)S(1)} %get-tuple-element.48), channel_id=1, source_target_pairs={{0,16},{8,24},{16,0},{24,8},{1,17},{9,25},{17,1},{25,9},{2,18},{10... | collective-permute-start | bytes 589832 | tf_op jit(solution)/shard_map/ppermute | solution.py:361
  72.4 13.8 %collective-permute-start.29 = (bf16[128,768]{1,0:T(8,128)(2,1)S(1)}, bf16[128,768]{1,0:T(8,128)(2,1)S(1)}, u32[]{:S(2)}, u32[]{:S(2)}) collective-permute-start(bf16[128,768]{1,0:T(8,128)(2,1)S(1)} %get-tuple-element.49), channel_id=1, source_target_pairs={{0,24},{8,16},{16,8},{24,0},{1,25},{9,17},{17,9},{25,1},{2,26},{10... | collective-permute-start | bytes 589832 | tf_op jit(solution)/shard_map/ppermute | solution.py:361
  86.3 8.8 %collective-permute-start.30 = (bf16[32,768]{1,0:T(8,128)(2,1)S(1)}, bf16[32,768]{1,0:T(8,128)(2,1)S(1)}, u32[]{:S(2)}, u32[]{:S(2)}) collective-permute-start(bf16[32,768]{1,0:T(8,128)(2,1)S(1)} %get-tuple-element.51), channel_id=1, source_target_pairs={{0,2},{1,3},{2,0},{3,1},{4,6},{5,7},{6,4},{7,5},{8,10},{9,11},{10,... | collective-permute-start | bytes 147464 | tf_op jit(solution)/shard_map/ppermute | solution.py:361
  88.4 11.0 %collective-permute-start.31 = (bf16[32,768]{1,0:T(8,128)(2,1)S(1)}, bf16[32,768]{1,0:T(8,128)(2,1)S(1)}, u32[]{:S(2)}, u32[]{:S(2)}) collective-permute-start(bf16[32,768]{1,0:T(8,128)(2,1)S(1)} %get-tuple-element.52), channel_id=1, source_target_pairs={{0,4},{1,5},{2,6},{3,7},{4,0},{5,1},{6,2},{7,3},{8,12},{9,13},{10,... | collective-permute-start | bytes 147464 | tf_op jit(solution)/shard_map/ppermute | solution.py:361
  89.4 10.0 %collective-permute-start.32 = (bf16[32,768]{1,0:T(8,128)(2,1)S(1)}, bf16[32,768]{1,0:T(8,128)(2,1)S(1)}, u32[]{:S(2)}, u32[]{:S(2)}) collective-permute-start(bf16[32,768]{1,0:T(8,128)(2,1)S(1)} %get-tuple-element.53), channel_id=1, source_target_pairs={{0,6},{1,7},{2,4},{3,5},{4,2},{5,3},{6,0},{7,1},{8,14},{9,15},{10,... | collective-permute-start | bytes 147464 | tf_op jit(solution)/shard_map/ppermute | solution.py:361
  90.1 9.3 %collective-permute-start.24 = (bf16[32,1280]{1,0:T(8,128)(2,1)S(1)}, bf16[32,1280]{1,0:T(8,128)(2,1)S(1)}, u32[]{:S(2)}, u32[]{:S(2)}) collective-permute-start(bf16[32,1280]{1,0:T(8,128)(2,1)S(1)} %get-tuple-element.43), channel_id=1, source_target_pairs={{0,8},{8,0},{16,24},{24,16},{1,9},{9,1},{17,25},{25,17},{2,10},{10... | collective-permute-start | bytes 245768 | tf_op jit(solution)/shard_map/ppermute | solution.py:361
  93.9 7.7 %collective-permute-start.25 = (bf16[32,1280]{1,0:T(8,128)(2,1)S(1)}, bf16[32,1280]{1,0:T(8,128)(2,1)S(1)}, u32[]{:S(2)}, u32[]{:S(2)}) collective-permute-start(bf16[32,1280]{1,0:T(8,128)(2,1)S(1)} %get-tuple-element.44), channel_id=1, source_target_pairs={{0,16},{8,24},{16,0},{24,8},{1,17},{9,25},{17,1},{25,9},{2,18},{10... | collective-permute-start | bytes 245768 | tf_op jit(solution)/shard_map/ppermute | solution.py:361
  95.1 6.6 %collective-permute-start.26 = (bf16[32,1280]{1,0:T(8,128)(2,1)S(1)}, bf16[32,1280]{1,0:T(8,128)(2,1)S(1)}, u32[]{:S(2)}, u32[]{:S(2)}) collective-permute-start(bf16[32,1280]{1,0:T(8,128)(2,1)S(1)} %get-tuple-element.45), channel_id=1, source_target_pairs={{0,24},{8,16},{16,8},{24,0},{1,25},{9,17},{17,9},{25,1},{2,26},{10... | collective-permute-start | bytes 245768 | tf_op jit(solution)/shard_map/ppermute | solution.py:361
  (4 other events, 69.6 us)
